TPU v7x, 32 devices: a whole 2x2x4 slice. The times are simulated.
32 devices in a mesh: ri: 8 (over z, core), rj: 4 (over y, x).
Axes of the slice: x: 2, y: 2, z: 4, core: 2. Of those that a mesh axis runs over, the one named last changes fastest.
Arguments:
- pair: bfloat16 [320, 320, 128], P('ri', 'rj'), may hold values from -6 to 6
- in_gain: float32 [128], replicated, may hold values from 0.1 to 1.9
- in_bias: float32 [128], replicated, may hold values from -3 to 3
- w_in: bfloat16 [128, 512], replicated, may hold values from -0.5 to 0.5
- w_gate: bfloat16 [128, 128], replicated, may hold values from -0.5 to 0.5
- out_gain: float32 [128], replicated, may hold values from 0.1 to 1.9
- out_bias: float32 [128], replicated, may hold values from -3 to 3
- w_out: bfloat16 [128, 128], replicated, may hold values from -0.5 to 0.5
Outputs:
- update: bfloat16 [320, 320, 128], P('ri', 'rj')
All inputs are finite; a program needn't handle non-finite values.
Results may differ from a plain program's by a relative error of at most 0.015.
Values may be sent and summed in bfloat16 or wider, within the bound.
A program may use at most 128 MiB of HBM per device.

v0:
```python
import jax
import jax.numpy as jnp
from jax import lax
from jax.sharding import PartitionSpec as P


def layer_norm(values, gain, bias):
    mean = jnp.mean(values, axis=-1, keepdims=True)
    centered = values - mean
    var = jnp.mean(centered * centered, axis=-1, keepdims=True)
    return centered * lax.rsqrt(var + 1e-05) * gain + bias


def local(pair, in_gain, in_bias, w_in, w_gate, out_gain, out_bias, w_out):
    rows, cols, chans = pair.shape
    hidden = w_out.shape[0]
    normed = layer_norm(pair.astype(jnp.float32), in_gain, in_bias).astype(jnp.bfloat16)
    flat = normed.reshape(rows * cols, chans)
    proj = jnp.dot(flat, w_in, preferred_element_type=jnp.float32)
    a_tile = (
        (jax.nn.sigmoid(proj[:, hidden : 2 * hidden]) * proj[:, :hidden])
        .astype(jnp.bfloat16)
        .reshape(rows, cols, hidden)
    )
    b_tile = (
        (jax.nn.sigmoid(proj[:, 3 * hidden :]) * proj[:, 2 * hidden : 3 * hidden])
        .astype(jnp.bfloat16)
        .reshape(rows, cols, hidden)
    )
    gate = jax.nn.sigmoid(jnp.dot(flat, w_gate, preferred_element_type=jnp.float32)).astype(
        jnp.bfloat16
    )
    a_rows = lax.all_gather(a_tile, "rj", axis=1, tiled=True)
    product = lax.dot_general(
        a_rows, b_tile, (((0,), (0,)), ((2,), (2,))), preferred_element_type=jnp.float32
    )
    summed = lax.psum_scatter(
        jnp.transpose(product, (1, 2, 0)).astype(jnp.bfloat16),
        "ri",
        scatter_dimension=0,
        tiled=True,
    ).astype(jnp.float32)
    tri = summed.reshape(rows * cols, hidden)
    tri_normed = layer_norm(tri, out_gain, out_bias).astype(jnp.bfloat16)
    mixed = jnp.dot(tri_normed, w_out, preferred_element_type=jnp.float32)
    update = gate.astype(jnp.float32) * mixed
    return update.reshape(rows, cols, chans).astype(jnp.bfloat16)


def solution(mesh):
    return jax.shard_map(
        local,
        mesh=mesh,
        in_specs=(P("ri", "rj", None), P(), P(), P(), P(), P(), P(), P()),
        out_specs=P("ri", "rj", None),
        check_vma=False,
    )
```

profile of v0, /device:TPU:1, one launch (start us, length us, event | category | flops | bytes accessed | tf_op | source)
XLA Modules:
  0.0 172.1 jit_solution(12855295967835624654)
XLA Ops:
  6.5 0.0 copy-start
  6.5 0.0 copy-start.1
  6.5 0.0 copy-start.4
  6.5 0.0 copy-start.5
  6.5 0.0 all-gather.2.cloned.1.call-start
  6.6 1.6 convert_reduce_fusion
  8.2 2.3 %fusion.8 = f32[40,80]{1,0:T(8,128)S(1)} fusion(bf16[40,80,128]{2,1,0:T(8,128)(2,1)} %param.8, f32[40,80]{1,0:T(8,128)S(1)} %broadcast_multiply_fusion.1), kind=kLoop, calls=%fused_computation.13 | loop fusion | flops 1635200 | bytes 844800 | tf_op jit(solution)/shard_map/reduce_sum | solution.py:10
  10.6 0.0 copy-done.1
  10.6 0.0 copy-done.4
  10.6 0.0 copy-done.5
  10.6 1.1 fusion.11
  11.7 0.0 copy-done
  11.7 1.0 fusion.24
  12.7 0.9 fusion.12
  13.6 1.1 copy.28
  14.7 0.0 all-gather.2.cloned.1.call-update
  14.7 0.0 reduce-scatter.2.cloned.1.call-start
  14.8 1.6 copy.30
  16.4 45.3 %all-gather.2.cloned.1.call-done = bf16[40,320,128]{2,0,1:T(8,128)(2,1)} async-done(((bf16[40,80,128]{2,0,1:T(8,128)(2,1)}), bf16[40,320,128]{2,0,1:T(8,128)(2,1)}) %all-gather.2.cloned.1.call-update) | async-done | bytes 3276816 | tf_op jit(solution)/shard_map/all_gather | solution.py:33
  61.7 6.7 %copy.29 = bf16[40,320,128]{1,0,2:T(8,128)(2,1)} copy(bf16[40,320,128]{2,0,1:T(8,128)(2,1)} %all-gather.2.cloned.1.call-done) | data formatting | bytes 6553600 | tf_op jit(solution)/shard_map/all_gather | solution.py:33
  68.5 7.4 %convert_bitcast_fusion = bf16[320,80,128]{0,1,2:T(8,128)(2,1)} fusion(bf16[40,320,128]{1,0,2:T(8,128)(2,1)} %copy.29, bf16[40,80,128]{1,0,2:T(8,128)(2,1)S(1)} %copy.30), kind=kOutput, calls=%fused_computation | convolution fusion | flops 265420800 | bytes 10649600 | tf_op jit(solution)/shard_map/dot_general | solution.py:34
  75.9 11.5 %copy.31 = bf16[320,80,128]{2,1,0:T(8,128)(2,1)} copy(bf16[320,80,128]{0,1,2:T(8,128)(2,1)} %convert_bitcast_fusion) | data formatting | bytes 13107200 | tf_op jit(solution)/shard_map/convert_element_type | solution.py:38
  87.4 0.0 copy-start.8
  87.4 0.0 reduce-scatter.2.cloned.1.call-update
  87.4 0.7 copy-done.8
  88.1 0.6 fusion.4
  88.7 0.0 copy-start.6
  88.7 0.0 copy-start.7
  88.7 0.0 copy-start.3
  88.8 69.3 %reduce-scatter.2.cloned.1.call-done = bf16[40,80,128]{2,1,0:T(8,128)(2,1)} async-done(((bf16[320,80,128]{2,1,0:T(8,128)(2,1)}), bf16[40,80,128]{2,1,0:T(8,128)(2,1)}) %reduce-scatter.2.cloned.1.call-update) | async-done | bytes 819216 | tf_op jit(solution)/shard_map/reduce_scatter | solution.py:37
  158.1 0.0 copy-start.2
  158.1 1.6 convert_reduce_fusion.1
  159.7 0.1 div.29
  159.8 2.3 %multiply_reduce_fusion = f32[40,80]{1,0:T(8,128)S(1)} fusion(f32[40,80]{1,0:T(8,128)S(1)} %broadcast_multiply_fusion, bf16[40,80,128]{2,1,0:T(8,128)(2,1)} %reduce-scatter.2.cloned.1.call-done), kind=kLoop, calls=%fused_computation.34 | loop fusion | flops 1635200 | bytes 844800 | tf_op jit(solution)/shard_map/reduce_sum | solution.py:10
  162.2 0.1 rsqrt.21
  162.2 0.0 copy-done.6
  162.2 0.0 copy-done.7
  162.2 0.0 copy-done.2
  162.2 1.7 %fusion.23 = bf16[3200,128]{1,0:T(8,128)(2,1)S(1)} fusion(f32[128]{0:T(128)S(1)} %copy-done.6, f32[128]{0:T(128)S(1)} %copy-done.7, f32[3200]{0:T(1024)S(1)} %rsqrt.21, f32[3200]{0:T(1024)S(1)} %div.29, bf16[40,80,128]{2,1,0:T(8,128)(2,1)S(1)} %copy-done.2), kind=kLoop, calls=%fused_computation.33 | loop fusion | flops 2457600 | bytes 1665024 | tf_op jit(solution)/shard_map/convert_element_type | solution.py:44
  164.0 0.0 copy-done.3
  164.0 1.3 fusion.5
  (4 shorter events, 0.0 us)
Async XLA Ops:
  6.5 5.2 %copy-start = (bf16[128,512]{1,0:T(8,128)(2,1)S(1)}, bf16[128,512]{1,0:T(8,128)(2,1)}, u32[]{:S(2)}) copy-start(bf16[128,512]{1,0:T(8,128)(2,1)} %param.11) | copy-start | bytes 393220
  6.5 4.1 %copy-start.1 = (bf16[40,80,128]{2,1,0:T(8,128)(2,1)S(1)}, bf16[40,80,128]{2,1,0:T(8,128)(2,1)}, u32[]{:S(2)}) copy-start(bf16[40,80,128]{2,1,0:T(8,128)(2,1)} %param.8) | copy-start | bytes 2457604
  6.5 4.1 %copy-start.4 = (f32[128]{0:T(128)S(1)}, f32[128]{0:T(128)}, u32[]{:S(2)}) copy-start(f32[128]{0:T(128)} %param.10) | copy-start | bytes 1540
  6.5 4.1 %copy-start.5 = (f32[128]{0:T(128)S(1)}, f32[128]{0:T(128)}, u32[]{:S(2)}) copy-start(f32[128]{0:T(128)} %param.9) | copy-start | bytes 1540
  6.5 55.2 %all-gather.2.cloned.1.call-start = ((), (), s32[]{:S(2)}) async-start(), calls=%async_computation.1 | async-start | bytes 4096000 | tf_op jit(solution)/shard_map/all_gather | solution.py:33
  14.7 143.3 %reduce-scatter.2.cloned.1.call-start = ((), (), s32[]{:S(2)}) async-start(), calls=%async_computation.2 | async-start | bytes 7372800 | tf_op jit(solution)/shard_map/reduce_scatter | solution.py:37
  87.4 0.8 copy-start.8
  88.7 73.5 %copy-start.6 = (f32[128]{0:T(128)S(1)}, f32[128]{0:T(128)}, u32[]{:S(2)}) copy-start(f32[128]{0:T(128)} %param.14) | copy-start | bytes 1540
  88.7 73.5 %copy-start.7 = (f32[128]{0:T(128)S(1)}, f32[128]{0:T(128)}, u32[]{:S(2)}) copy-start(f32[128]{0:T(128)} %param.13) | copy-start | bytes 1540
  88.7 75.3 %copy-start.3 = (bf16[128,128]{1,0:T(8,128)(2,1)S(1)}, bf16[128,128]{1,0:T(8,128)(2,1)}, u32[]{:S(2)}) copy-start(bf16[128,128]{1,0:T(8,128)(2,1)} %param.15) | copy-start | bytes 98308
  158.1 4.2 %copy-start.2 = (bf16[40,80,128]{2,1,0:T(8,128)(2,1)S(1)}, bf16[40,80,128]{2,1,0:T(8,128)(2,1)}, u32[]{:S(2)}) copy-start(bf16[40,80,128]{2,1,0:T(8,128)(2,1)} %reduce-scatter.2.cloned.1.call-done) | copy-start | bytes 2457604
Sparse Core Ops, SparseCore 0:
  14.8 46.8 all-gather.1
  87.5 70.4 reduce-scatter.1
where the time goes:
time: 175 us; the launch traced here: 172 us
  waiting for transfers between devices  115 us (66%)
  local copies, waits for them, and re-layouts  21.9 us (13%)
  between operations  13.6 us (8%)
  other arithmetic  11.7 us (7%)
  matrix products  10.3 us (6%)
    reduce_scatter x1, waiting for transfers between devices, local(): lax.psum_scatter(jnp.transpose(product, (1, 2, 0)).astype(jnp.bfloat16),...  69.3 us
    all_gather x1, waiting for transfers between devices, local(): a_rows = lax.all_gather(a_tile, 'rj', axis=1, tiled=True)  45.3 us
    convert_element_type x1, local copies, waits for them, and re-layouts, local(): jnp.transpose(product, (1, 2, 0)).astype(jnp.bfloat16)  11.5 us
    dot_general x1, matrix products, local(): lax.dot_general(a_rows, b_tile, (((0,), (0,)), ((2,), (2,))), preferred_e...  7.43 us
    all_gather x1, local copies, waits for them, and re-layouts, local(): a_rows = lax.all_gather(a_tile, 'rj', axis=1, tiled=True)  6.75 us
    reduce_sum x2, other arithmetic, layer_norm(): var = jnp.mean(centered * centered, axis=-1, keepdims=True)  4.67 us
  transfers between devices with their start and end apart: 2, of which 2 were waited for; matrix products, arithmetic and copies ran while one was open for 1% of the time, Pallas kernels for 0%

commit v1 on v0

v1 whole, which is shorter than its diff:
```python
import jax
import jax.numpy as jnp
from jax import lax
from jax.sharding import PartitionSpec as P

AXES = ("ri", "rj")


def layer_norm(values, gain, bias, axis):
    mean = jnp.mean(values, axis=axis, keepdims=True)
    centered = values - mean
    var = jnp.mean(centered * centered, axis=axis, keepdims=True)
    return centered * lax.rsqrt(var + 1e-05) * gain + bias


def exchange(blocks):
    return lax.all_to_all(blocks, AXES, 0, 0, tiled=True)


def local(n_ri, n_rj, pair, in_gain, in_bias, w_in, w_gate, out_gain, out_bias, w_out):
    rows, cols, chans = pair.shape
    hidden = w_out.shape[0]
    n = n_ri * n_rj
    own = hidden // n
    spots = rows * cols
    flat = layer_norm(
        pair.reshape(spots, chans).astype(jnp.float32), in_gain, in_bias, -1
    ).astype(jnp.bfloat16)
    proj = lax.dot_general(
        w_in, flat, (((0,), (1,)), ((), ())), preferred_element_type=jnp.float32
    ).reshape(4, n, own, spots)
    a_blocks = (jax.nn.sigmoid(proj[1]) * proj[0]).astype(jnp.bfloat16)
    b_blocks = (jax.nn.sigmoid(proj[3]) * proj[2]).astype(jnp.bfloat16)
    got = exchange(jnp.concatenate([a_blocks, b_blocks], axis=1))
    gate = jax.nn.sigmoid(jnp.dot(flat, w_gate, preferred_element_type=jnp.float32)).astype(
        jnp.bfloat16
    )
    got = got.reshape(n_ri, n_rj, 2, own, rows, cols)
    got = jnp.transpose(got, (2, 3, 0, 4, 1, 5)).reshape(2, own, n_ri * rows, n_rj * cols)
    product = lax.dot_general(
        got[0], got[1], (((1,), (1,)), ((0,), (0,))), preferred_element_type=jnp.float32
    ).astype(jnp.bfloat16)
    product = product.reshape(own, n_ri, rows, n_rj, cols)
    product = jnp.transpose(product, (1, 3, 0, 2, 4)).reshape(n, own, spots)
    tri = exchange(product).reshape(hidden, spots).astype(jnp.float32)
    tri_normed = layer_norm(tri, out_gain[:, None], out_bias[:, None], 0).astype(jnp.bfloat16)
    mixed = lax.dot_general(
        tri_normed, w_out, (((0,), (0,)), ((), ())), preferred_element_type=jnp.float32
    )
    update = gate.astype(jnp.float32) * mixed
    return update.reshape(rows, cols, chans).astype(jnp.bfloat16)


def solution(mesh):
    n_ri, n_rj = mesh.shape["ri"], mesh.shape["rj"]
    return jax.shard_map(
        lambda *args: local(n_ri, n_rj, *args),
        mesh=mesh,
        in_specs=(P("ri", "rj", None), P(), P(), P(), P(), P(), P(), P()),
        out_specs=P("ri", "rj", None),
        check_vma=False,
    )
```

time: 175 us -> 105 us (0.60)
  waiting for transfers between devices: 115 us -> 19.4 us
  blocking collectives: 0 us -> 45.9 us
  between operations: 13.6 us -> 0.26 us
  local copies, waits for them, and re-layouts: 21.9 us -> 17.4 us
  starting transfers between devices: 0.08 us -> 3.66 us
  other arithmetic: 11.7 us -> 8.3 us
    reduce_scatter x1 -> x0, waiting for transfers between devices: 69.3 us -> none  [local(): lax.psum_scatter(jnp.transpose(product, (1, 2, 0)).astype(jnp.bfloat16),...]
    all_to_all x0 -> x1, blocking collectives: none -> 45.9 us  [exchange(): return lax.all_to_all(blocks, AXES, 0, 0, tiled=True)]
    all_gather x1 -> x0, waiting for transfers between devices: 45.3 us -> none  [local(): a_rows = lax.all_gather(a_tile, 'rj', axis=1, tiled=True)]
    all_to_all x0 -> x1, waiting for transfers between devices: none -> 19.4 us  [exchange(): return lax.all_to_all(blocks, AXES, 0, 0, tiled=True)]
    convert_element_type x1 -> x3, local copies, waits for them, and re-layouts: 11.5 us -> 0.48 us  [the longest x1 0.19 us: local(): a_blocks = (jax.nn.sigmoid(proj[1]) * proj[0]).astype(jnp.bfloat16)]
    reshape x2 -> x5, local copies, waits for them, and re-layouts: 2.7 us -> 9.52 us  [the longest x1 4.12 us: local(): got = got.reshape(n_ri, n_rj, 2, own, rows, cols)]
    all_gather x1 -> x0, local copies, waits for them, and re-layouts: 6.75 us -> none  [local(): a_rows = lax.all_gather(a_tile, 'rj', axis=1, tiled=True)]
    all_to_all x0 -> x1, starting transfers between devices: none -> 3.66 us  [exchange(): return lax.all_to_all(blocks, AXES, 0, 0, tiled=True)]
  transfers between devices with their start and end apart: 2 -> 1, of which waited for: 2 -> 1; matrix products, arithmetic and copies ran while one was open for 1% -> 2% of each run, Pallas kernels for 0% -> 0%
where the time goes in v1:
time: 105 us; the launch traced here: 104 us
  blocking collectives  45.9 us (44%)
  waiting for transfers between devices  19.4 us (18%)
  local copies, waits for them, and re-layouts  17.4 us (17%)
  matrix products  8.68 us (8%)
  other arithmetic  8.3 us (8%)
  starting transfers between devices  3.66 us (3%)
    all_to_all x1, blocking collectives, exchange(): return lax.all_to_all(blocks, AXES, 0, 0, tiled=True)  45.9 us
    all_to_all x1, waiting for transfers between devices, exchange(): return lax.all_to_all(blocks, AXES, 0, 0, tiled=True)  19.4 us
    reshape x1, local copies, waits for them, and re-layouts, local(): got = got.reshape(n_ri, n_rj, 2, own, rows, cols)  4.12 us
    all_to_all x1, starting transfers between devices, exchange(): return lax.all_to_all(blocks, AXES, 0, 0, tiled=True)  3.66 us
    reshape x2, local copies, waits for them, and re-layouts, local(): product = product.reshape(own, n_ri, rows, n_rj, cols)  3.14 us
    dot_general x1, matrix products, local(): lax.dot_general(got[0], got[1], (((1,), (1,)), ((0,), (0,))), preferred_e...  3.01 us
    reduce_sum x2, other arithmetic, layer_norm(): var = jnp.mean(centered * centered, axis=axis, keepdims=True)  2.89 us
    dot_general x1, matrix products, local(): lax.dot_general(tri_normed, w_out, (((0,), (0,)), ((), ())), preferred_el...  2.86 us
  transfers between devices with their start and end apart: 1, of which 1 were waited for; matrix products, arithmetic and copies ran while one was open for 2% of the time, Pallas kernels for 0%

profile of v1, /device:TPU:1, one launch (start us, length us, event | category | flops | bytes accessed | tf_op | source)
XLA Modules:
  0.0 103.7 jit_solution(17636159072968994661)
XLA Ops:
  0.0 0.0 copy-start
  0.0 0.0 copy-start.8
  0.0 1.6 %convert_reduce_fusion.1 = f32[40,80]{1,0:T(8,128)S(1)} fusion(bf16[40,80,128]{2,1,0:T(8,128)(2,1)} %param.8), kind=kLoop, calls=%fused_computation.33 | loop fusion | flops 816000 | bytes 832000 | tf_op jit(solution)/shard_map/reduce_sum | solution.py:10
  1.7 2.3 %multiply_reduce_fusion.1 = f32[40,80]{1,0:T(8,128)S(1)} fusion(bf16[40,80,128]{2,1,0:T(8,128)(2,1)} %param.8, f32[40,80]{1,0:T(8,128)S(1)} %broadcast_multiply_fusion), kind=kLoop, calls=%fused_computation.29 | loop fusion | flops 1635200 | bytes 844800 | tf_op jit(solution)/shard_map/reduce_sum | solution.py:12
  4.0 0.1 div.30
  4.1 0.1 rsqrt.20
  4.2 0.0 copy-done.1
  4.2 0.0 copy-done.7
  4.2 0.0 copy-done.8
  4.2 1.7 %fusion.17 = bf16[3200,128]{1,0:T(8,128)(2,1)S(1)} fusion(bf16[40,80,128]{2,1,0:T(8,128)(2,1)S(1)} %copy-done.1, f32[128]{0:T(128)S(1)} %copy-done.7, f32[128]{0:T(128)S(1)} %copy-done.8, f32[3200]{0:T(1024)S(1)} %rsqrt.20, f32[3200]{0:T(1024)S(1)} %div.30), kind=kLoop, calls=%fused_computation.26 | loop fusion | flops 2457600 | bytes 1665024 | tf_op jit(solution)/shard_map/convert_element_type | solution.py:28
  6.0 0.0 copy-start.2
  6.0 0.9 copy-done.2
  6.9 0.0 copy-done
  6.9 1.1 %convolution_bitcast_fusion = f32[512,3200]{1,0:T(8,128)S(1)} fusion(bf16[3200,128]{1,0:T(8,128)(2,1)S(1)} %fusion.17, bf16[128,512]{1,0:T(8,128)(2,1)S(1)} %copy-done), kind=kOutput, calls=%fused_computation | convolution fusion | flops 419430400 | bytes 7503872 | tf_op jit(solution)/shard_map/dot_general | solution.py:29
  7.9 0.9 fusion.10
  8.8 0.2 reshape.103
  9.0 0.2 reshape.104
  9.2 0.8 pad_maximum_fusion
  10.0 45.9 %all_to_all.10 = bf16[32,8,3200]{2,1,0:T(8,128)(2,1)} all-to-all(bf16[32,8,3200]{2,1,0:T(8,128)(2,1)S(1)} %pad_maximum_fusion), channel_id=1, replica_groups=mesh['ri'=8,'rj'=4] {'ri','rj'}, dimensions={0} | all-to-all | bytes 3276800 | tf_op jit(solution)/shard_map/all_to_all | solution.py:17
  55.9 4.1 %reshape.96 = bf16[8,4,2,4,40,80]{5,4,3,2,1,0:T(8,128)(2,1)S(1)} reshape(bf16[32,8,3200]{2,1,0:T(8,128)(2,1)} %all_to_all.10) | data formatting | bytes 3276800 | tf_op jit(solution)/shard_map/reshape | solution.py:38
  60.0 1.5 %fusion.22 = (bf16[1,4,8,40,4,80]{5,3,1,0,4,2:T(8,128)(2,1)}, bf16[1,4,8,40,4,80]{5,3,1,0,4,2:T(8,128)(2,1)S(1)}) fusion(bf16[2,4,8,40,4,80]{5,3,1,0,4,2:T(8,128)(2,1)S(1)} %bitcast.28), kind=kLoop, calls=%fused_computation.42 | loop fusion | bytes 3276800 | tf_op jit(solution)/shard_map/slice | solution.py:41
  61.6 0.7 copy.18
  62.2 0.0 copy-start.4
  62.2 1.7 %reshape.106 = bf16[4,320,320]{2,1,0:T(8,128)(2,1)} reshape(bf16[1,4,8,40,4,80]{5,4,3,2,1,0:T(4,128)(2,1)S(1)} %copy.18) | data formatting | bytes 1638400 | tf_op jit(solution)/shard_map/squeeze | solution.py:41
  64.0 0.0 copy-done.4
  64.0 0.7 copy.19
  64.6 0.0 copy-start.5
  64.6 1.7 %squeeze.17 = bf16[4,320,320]{2,1,0:T(8,128)(2,1)} reshape(bf16[1,4,8,40,4,80]{5,4,3,2,1,0:T(4,128)(2,1)S(1)} %copy.19) | data formatting | bytes 1638400 | tf_op jit(solution)/shard_map/squeeze | solution.py:41
  66.3 0.0 copy-done.5
  66.3 3.0 %convolution_convert_fusion = bf16[4,320,320]{2,1,0:T(8,128)(2,1)} fusion(bf16[4,320,320]{2,1,0:T(8,128)(2,1)S(1)} %copy-done.5, bf16[4,320,320]{2,1,0:T(8,128)(2,1)} %squeeze.17), kind=kOutput, calls=%fused_computation.30 | convolution fusion | flops 262553600 | bytes 2457600 | tf_op jit(solution)/shard_map/dot_general | solution.py:40
  69.3 2.9 %reshape.97 = bf16[4,8,40,4,80]{4,3,2,1,0:T(4,128)(2,1)S(1)} reshape(bf16[4,320,320]{2,1,0:T(8,128)(2,1)} %convolution_convert_fusion) | data formatting | bytes 1638400 | tf_op jit(solution)/shard_map/reshape | solution.py:43
  72.3 0.2 copy.26
  72.5 1.0 reshape.98
  73.5 0.0 copy-start.3
  73.5 0.0 copy-start.11
  73.5 1.3 %copy.22 = bf16[32,4,3200]{2,1,0:T(4,128)(2,1)} copy(bf16[32,4,3200]{2,0,1:T(8,128)(2,1)S(1)} %reshape.98) | data formatting | bytes 1638400 | tf_op jit(solution)/shard_map/reshape | solution.py:44
  74.8 3.7 %all-to-all-start.1 = ((bf16[32,4,3200]{2,1,0:T(4,128)(2,1)}), bf16[32,4,3200]{2,1,0:T(4,128)(2,1)S(1)}, u32[]{:S(2)}, u32[]{:S(2)}) async-start(bf16[32,4,3200]{2,1,0:T(4,128)(2,1)} %copy.22), calls=%async_computation.1 | async-start | bytes 1638400 | tf_op jit(solution)/shard_map/all_to_all | solution.py:17
  78.5 0.0 copy-done.3
  78.5 1.7 %fusion.4 = f32[3200,128]{1,0:T(8,128)} fusion(bf16[3200,128]{1,0:T(8,128)(2,1)S(1)} %copy-done.3, bf16[128,128]{1,0:T(8,128)(2,1)S(1)} %copy-done.11), kind=kOutput, calls=%fused_computation.7 | convolution fusion | flops 106905600 | bytes 2490368 | tf_op jit(solution)/shard_map/dot_general | solution.py:35
  80.2 19.4 %all-to-all-done.1 = bf16[32,4,3200]{2,1,0:T(4,128)(2,1)S(1)} async-done(((bf16[32,4,3200]{2,1,0:T(4,128)(2,1)}), bf16[32,4,3200]{2,1,0:T(4,128)(2,1)S(1)}, u32[]{:S(2)}, u32[]{:S(2)}) %all-to-all-start.1) | async-done | bytes 819232 | tf_op jit(solution)/shard_map/all_to_all | solution.py:17
  99.7 0.3 convert_reduce_fusion
  100.0 0.0 copy-start.6
  100.0 0.0 copy-start.9
  100.1 0.0 copy-start.10
  100.1 0.6 multiply_reduce_fusion
  100.6 0.1 reshape.102
  100.8 0.0 copy-done.6
  100.8 2.9 %fusion.5 = bf16[3200,128]{1,0:T(8,128)(2,1)} fusion(f32[3200,128]{1,0:T(8,128)} %fusion.4, bf16[128,128]{1,0:T(8,128)(2,1)S(1)} %copy-done.6, f32[128,3200]{1,0:T(8,128)S(1)} %reshape.102, f32[128]{0:T(128)S(1)} %copy-done.9, f32[128]{0:T(128)S(1)} %copy-done.10, f32[3200]{0:T(1024)S(1)} %add_rsqrt_fusion.1, f32[3200]{0:T(1024)S(1)} %broadcast_multiply_fusion.1), kind=kOutput, calls=%fused_computation.8 | convolution fusion | flops 107724800 | bytes 4155392 | tf_op jit(solution)/shard_map/dot_general | solution.py:47
  (9 shorter events, 0.0 us)
Async XLA Ops:
  0.0 6.9 %copy-start = (bf16[128,512]{1,0:T(8,128)(2,1)S(1)}, bf16[128,512]{1,0:T(8,128)(2,1)}, u32[]{:S(2)}) copy-start(bf16[128,512]{1,0:T(8,128)(2,1)} %param.11) | copy-start | bytes 393220
  0.0 4.2 %copy-start.1 = (bf16[40,80,128]{2,1,0:T(8,128)(2,1)S(1)}, bf16[40,80,128]{2,1,0:T(8,128)(2,1)}, u32[]{:S(2)}) copy-start(bf16[40,80,128]{2,1,0:T(8,128)(2,1)} %param.8) | copy-start | bytes 2457604
  0.0 4.2 %copy-start.7 = (f32[128]{0:T(128)S(1)}, f32[128]{0:T(128)}, u32[]{:S(2)}) copy-start(f32[128]{0:T(128)} %param.10) | copy-start | bytes 1540
  0.0 4.2 %copy-start.8 = (f32[128]{0:T(128)S(1)}, f32[128]{0:T(128)}, u32[]{:S(2)}) copy-start(f32[128]{0:T(128)} %param.9) | copy-start | bytes 1540
  6.0 0.9 copy-start.2
  62.2 1.7 %copy-start.4 = (bf16[1,4,8,40,4,80]{5,3,1,0,4,2:T(8,128)(2,1)S(1)}, bf16[1,4,8,40,4,80]{5,3,1,0,4,2:T(8,128)(2,1)}, u32[]{:S(2)}) copy-start(bf16[1,4,8,40,4,80]{5,3,1,0,4,2:T(8,128)(2,1)} %get-tuple-element.7) | copy-start | bytes 2457604
  64.6 1.7 %copy-start.5 = (bf16[4,320,320]{2,1,0:T(8,128)(2,1)S(1)}, bf16[4,320,320]{2,1,0:T(8,128)(2,1)}, u32[]{:S(2)}) copy-start(bf16[4,320,320]{2,1,0:T(8,128)(2,1)} %reshape.106) | copy-start | bytes 2457604
  73.5 5.0 %copy-start.3 = (bf16[3200,128]{1,0:T(8,128)(2,1)S(1)}, bf16[3200,128]{1,0:T(8,128)(2,1)}, u32[]{:S(2)}) copy-start(bf16[3200,128]{1,0:T(8,128)(2,1)} %copy-done.2) | copy-start | bytes 2457604
  73.5 5.0 %copy-start.11 = (bf16[128,128]{1,0:T(8,128)(2,1)S(1)}, bf16[128,128]{1,0:T(8,128)(2,1)}, u32[]{:S(2)}) copy-start(bf16[128,128]{1,0:T(8,128)(2,1)} %param.12) | copy-start | bytes 98308
  74.8 24.9 %all-to-all-start.1 = ((bf16[32,4,3200]{2,1,0:T(4,128)(2,1)}), bf16[32,4,3200]{2,1,0:T(4,128)(2,1)S(1)}, u32[]{:S(2)}, u32[]{:S(2)}) async-start(bf16[32,4,3200]{2,1,0:T(4,128)(2,1)} %copy.22), calls=%async_computation.1 | async-start | bytes 1638400 | tf_op jit(solution)/shard_map/all_to_all | solution.py:17
  100.0 0.8 copy-start.6
  100.0 0.8 copy-start.9
  100.1 0.7 copy-start.10

commit v2 on v1

v2 whole, which is shorter than its diff:
```python
import functools

import jax
import jax.numpy as jnp
from jax import lax
from jax.experimental import pallas as pl
from jax.experimental.pallas import tpu as pltpu
from jax.sharding import PartitionSpec as P

MESH = pl.DeviceIdType.MESH
LANES = 128


def shifted(vregs, start):
    at, by = divmod(start, LANES)
    if by == 0:
        return vregs[at]
    return pltpu.roll(vregs[at], LANES - by, 1)


def body(n_ri, n_rj, rows, cols, own, pair, gain, bias, w_in, w_gate, gate_ref, out_ref,
         flat_s, ab_s, x_s, recv_s, g_s, b_s, o_s, t_s,
         send1, recv1, send2, recv2, loc):
    n = n_ri * n_rj
    spots = rows * cols
    depth = n_ri * rows
    hidden = n * own
    halves = cols // rows
    ri, rj = lax.axis_index("ri"), lax.axis_index("rj")
    me = ri * n_rj + rj

    def other(d):
        return lax.rem(me + d, n)

    barrier = pltpu.get_barrier_semaphore()

    def greet(d, _):
        to = other(d)
        pl.semaphore_signal(
            barrier, inc=1, device_id=(to // n_rj, lax.rem(to, n_rj)), device_id_type=MESH
        )
        return _

    lax.fori_loop(1, n, greet, 0)

    wt = w_in[...].T
    step = spots // 5

    def project(i, _):
        at = pl.multiple_of(i * step, LANES)
        x = pair[pl.ds(at, step), :].astype(jnp.float32)
        mean = jnp.mean(x, axis=-1, keepdims=True)
        centered = x - mean
        var = jnp.mean(centered * centered, axis=-1, keepdims=True)
        flat = (centered * lax.rsqrt(var + 1e-05) * gain[...] + bias[...]).astype(jnp.bfloat16)
        flat_s[pl.ds(at, step), :] = flat
        proj = lax.dot_general(
            wt, flat, (((1,), (1,)), ((), ())), preferred_element_type=jnp.float32
        )
        ab_s[0, :, pl.ds(at, step)] = (
            jax.nn.sigmoid(proj[hidden : 2 * hidden]) * proj[:hidden]
        )
        ab_s[1, :, pl.ds(at, step)] = (
            jax.nn.sigmoid(proj[3 * hidden :]) * proj[2 * hidden : 3 * hidden]
        )
        return _

    lax.fori_loop(0, 5, project, 0)

    each = 8 // own

    def split(p, _):
        at = pl.multiple_of(p * 8, 8)
        a8, b8 = ab_s[0, pl.ds(at, 8), :], ab_s[1, pl.ds(at, 8), :]
        for e in range(each):
            pick = slice(e * own, (e + 1) * own)
            x_s[p * each + e] = jnp.concatenate([a8[pick], b8[pick]], axis=0).astype(jnp.bfloat16)
        return _

    lax.fori_loop(0, hidden // 8, split, 0)
    pl.semaphore_wait(barrier, n - 1)

    def copy_in(d, src):
        return pltpu.make_async_remote_copy(
            src_ref=x_s.at[d], dst_ref=recv_s.at[src], send_sem=send1.at[d],
            recv_sem=recv1.at[src], device_id=(d // n_rj, lax.rem(d, n_rj)), device_id_type=MESH,
        )

    def copy_back(d, src):
        return pltpu.make_async_remote_copy(
            src_ref=t_s.at[d], dst_ref=out_ref.at[src], send_sem=send2.at[d],
            recv_sem=recv2.at[src], device_id=(d // n_rj, lax.rem(d, n_rj)), device_id_type=MESH,
        )

    def send(d, _):
        copy_in(other(d), me).start()
        return _

    lax.fori_loop(1, n, send, 0)

    def gates(i, _):
        at = pl.multiple_of(i * step, LANES)
        gate_ref[pl.ds(at, step), :] = jax.nn.sigmoid(
            jnp.dot(flat_s[pl.ds(at, step), :], w_gate[...], preferred_element_type=jnp.float32)
        ).astype(jnp.bfloat16)
        return _

    lax.fori_loop(0, 5, gates, 0)

    lane = lax.broadcasted_iota(jnp.int32, (2 * own, LANES), 1)

    def unpack(block, src):
        i0 = (src // n_rj) * rows
        j = lax.rem(src, n_rj)
        wide = block.astype(jnp.float32)
        vregs = [wide[:, v * LANES : (v + 1) * LANES] for v in range(spots // LANES)]
        for k in range(rows):
            start = k * cols
            val = shifted(vregs, start)
            have = LANES - start % LANES
            if have < cols:
                val = jnp.where(
                    lane < have, val, pltpu.roll(vregs[start // LANES + 1], have, 1)
                )
            g_s[j, pl.ds(i0 + k, 2 * own, stride=depth), :] = val

    unpack(x_s[me], me)

    def take(d, _):
        src = lax.rem(me + n - d, n)
        copy_in(src, src).wait_recv()
        unpack(recv_s[src], src)
        return _

    lax.fori_loop(1, n, take, 0)

    for c in range(own):
        for q in range(n_rj):
            b_s[c, :, q * LANES : (q + 1) * LANES] = g_s[
                q, (own + c) * depth : (own + c + 1) * depth, :
            ].astype(jnp.bfloat16)

    lane_o = lax.broadcasted_iota(jnp.int32, (own, LANES), 1)

    def emit(pp, _):
        p = lax.rem(pp + n_rj // 2 + ri // halves, n_rj)
        for c in range(own):
            lhs = g_s[p, c * depth : (c + 1) * depth, :].astype(jnp.bfloat16)
            product = lax.dot_general(
                lhs, b_s[c], (((0,), (0,)), ((), ())), preferred_element_type=jnp.float32
            )
            for q in range(n_rj):
                o_s[q, c * LANES : (c + 1) * LANES, :] = product[:, q * LANES : (q + 1) * LANES]

        def deliver(s, _):
            h, q = s // n_rj, lax.rem(s + rj, n_rj)
            d = (p * halves + h) * n_rj + q
            got = [
                o_s[q, pl.ds(h * rows + r, own, stride=LANES), :] for r in range(rows)
            ]
            pieces = []
            for v in range(spots // LANES):
                piece = None
                for r in range((v * LANES) // cols, min(rows, ((v + 1) * LANES - 1) // cols + 1)):
                    at = r * cols - v * LANES
                    val = pltpu.roll(got[r], at % LANES, 1) if at % LANES else got[r]
                    piece = val if piece is None else jnp.where(lane_o >= at, val, piece)
                pieces.append(piece)
            t_s[d] = jnp.concatenate(pieces, axis=1).astype(jnp.bfloat16)

            @pl.when(d != me)
            def start():
                copy_back(d, me).start()

            return _

        lax.fori_loop(0, halves * n_rj, deliver, 0)
        return _

    lax.fori_loop(0, n_rj, emit, 0)
    mine = pltpu.make_async_copy(t_s.at[me], out_ref.at[me], loc)
    mine.start()

    def finish(d, _):
        src = lax.rem(me + n - d, n)
        to = other(d)
        copy_in(to, me).wait_send()
        copy_back(to, me).wait_send()
        copy_back(src, src).wait_recv()
        return _

    lax.fori_loop(1, n, finish, 0)
    mine.wait()


def exchange(n_ri, n_rj, rows, cols, own, pair, gain, bias, w_in, w_gate):
    n = n_ri * n_rj
    spots, chans = pair.shape
    depth = n_ri * rows
    hidden = n * own
    vmem = pl.BlockSpec(memory_space=pltpu.VMEM)
    return pl.pallas_call(
        functools.partial(body, n_ri, n_rj, rows, cols, own),
        out_shape=(
            jax.ShapeDtypeStruct((spots, chans), jnp.bfloat16),
            jax.ShapeDtypeStruct((n, own, spots), jnp.bfloat16),
        ),
        in_specs=[vmem] * 5,
        out_specs=(vmem, vmem),
        scratch_shapes=[
            pltpu.VMEM((spots, chans), jnp.bfloat16),
            pltpu.VMEM((2, hidden, spots), jnp.float32),
            pltpu.VMEM((n, 2 * own, spots), jnp.bfloat16),
            pltpu.VMEM((n, 2 * own, spots), jnp.bfloat16),
            pltpu.VMEM((n_rj, 2 * own * depth, LANES), jnp.float32),
            pltpu.VMEM((own, depth, n_rj * LANES), jnp.bfloat16),
            pltpu.VMEM((n_rj, own * LANES, LANES), jnp.float32),
            pltpu.VMEM((n, own, spots), jnp.bfloat16),
            pltpu.SemaphoreType.DMA((n,)),
            pltpu.SemaphoreType.DMA((n,)),
            pltpu.SemaphoreType.DMA((n,)),
            pltpu.SemaphoreType.DMA((n,)),
            pltpu.SemaphoreType.DMA,
        ],
        compiler_params=pltpu.CompilerParams(
            collective_id=0, has_side_effects=True, vmem_limit_bytes=56 << 20
        ),
    )(pair, gain, bias, w_in, w_gate)


def local(n_ri, n_rj, pair, in_gain, in_bias, w_in, w_gate, out_gain, out_bias, w_out):
    rows, cols, chans = pair.shape
    hidden = w_out.shape[0]
    n = n_ri * n_rj
    own = hidden // n
    spots = rows * cols
    gate, tri = exchange(
        n_ri, n_rj, rows, cols, own, pair.reshape(spots, chans),
        in_gain[None], in_bias[None], w_in, w_gate,
    )
    tri = tri.reshape(hidden, spots).astype(jnp.float32)
    mean = jnp.mean(tri, axis=0, keepdims=True)
    centered = tri - mean
    var = jnp.mean(centered * centered, axis=0, keepdims=True)
    tri_normed = (
        centered * lax.rsqrt(var + 1e-05) * out_gain[:, None] + out_bias[:, None]
    ).astype(jnp.bfloat16)
    mixed = lax.dot_general(
        tri_normed, w_out, (((0,), (0,)), ((), ())), preferred_element_type=jnp.float32
    )
    update = gate.astype(jnp.float32) * mixed
    return update.reshape(rows, cols, chans).astype(jnp.bfloat16)


def solution(mesh):
    n_ri, n_rj = mesh.shape["ri"], mesh.shape["rj"]
    return jax.shard_map(
        lambda *args: local(n_ri, n_rj, *args),
        mesh=mesh,
        in_specs=(P("ri", "rj", None), P(), P(), P(), P(), P(), P(), P()),
        out_specs=P("ri", "rj", None),
        check_vma=False,
    )
```

time: 105 us -> 78.1 us (0.74); the launches traced: 104 us -> 77.9 us
  Pallas kernels: 0 us -> 72.9 us
  blocking collectives: 45.9 us -> 0 us
  waiting for transfers between devices: 19.4 us -> 0 us
  local copies, waits for them, and re-layouts: 17.4 us -> 0.13 us
  matrix products: 8.68 us -> 1.44 us
  other arithmetic: 8.3 us -> 3.34 us
  starting transfers between devices: 3.66 us -> 0 us
    pallas_call x0 -> x1, Pallas kernels: none -> 72.9 us  [exchange(): pl.pallas_call(functools.partial(body, n_ri, n_rj, rows, cols, own), out_...]
    all_to_all x1 -> x0, blocking collectives: 45.9 us -> none  [exchange(): return lax.all_to_all(blocks, AXES, 0, 0, tiled=True)]
    all_to_all x1 -> x0, waiting for transfers between devices: 19.4 us -> none  [exchange(): return lax.all_to_all(blocks, AXES, 0, 0, tiled=True)]
    reshape x5 -> x0, local copies, waits for them, and re-layouts: 9.52 us -> none  [the longest x1 4.12 us: local(): got = got.reshape(n_ri, n_rj, 2, own, rows, cols)]
    dot_general x3 -> x0, matrix products: 5.82 us -> none  [the longest x1 3.01 us: local(): lax.dot_general(got[0], got[1], (((1,), (1,)), ((0,), (0,))), preferred_e...]
    all_to_all x1 -> x0, starting transfers between devices: 3.66 us -> none  [exchange(): return lax.all_to_all(blocks, AXES, 0, 0, tiled=True)]
    squeeze x2 -> x0, local copies, waits for them, and re-layouts: 3.4 us -> none  [the longest x1 1.72 us: local(): got[0]]
    slice x3 -> x0, local copies, waits for them, and re-layouts: 2.88 us -> none  [the longest x2 2.2 us: local(): got[1]]
  transfers between devices with their start and end apart: 1 -> 0, of which waited for: 1 -> 0; matrix products, arithmetic and copies ran while one was open for 2% -> 0% of each run, Pallas kernels for 0% -> 0%
where the time goes in v2:
time: 78.1 us; the launch traced here: 77.9 us
  Pallas kernels  72.9 us (93%)
  other arithmetic  3.34 us (4%)
  matrix products  1.44 us (2%)
    pallas_call x1, Pallas kernels, exchange(): pl.pallas_call(functools.partial(body, n_ri, n_rj, rows, cols, own), out_...  72.9 us
    reduce_sum x1, other arithmetic, local(): var = jnp.mean(centered * centered, axis=0, keepdims=True)  1.77 us

profile of v2, /device:TPU:1, one launch (start us, length us, event | category | flops | bytes accessed | tf_op | source)
XLA Modules:
  0.0 77.9 jit_solution(13768716741490732449)
XLA Ops:
  0.0 0.0 copy-start
  0.0 72.9 %shard_map.82 = (bf16[3200,128]{1,0:T(8,128)(2,1)}, bf16[32,4,3200]{2,1,0:T(4,128)(2,1)}) custom-call(bf16[3200,128]{1,0:T(8,128)(2,1)} %bitcast.5, f32[1,128]{1,0:T(1,128)} %bitcast.6, f32[1,128]{1,0:T(1,128)} %bitcast.7, bf16[128,512]{1,0:T(8,128)(2,1)} %w_in.1, bf16[128,128]{1,0:T(8,128)(2,1)} %w_gate.1), custom_call_target="tpu_custom_call" | custom-call | tf_op jit(solution)/shard_map/pallas_call | solution.py:202
  72.9 0.0 copy-start.1
  72.9 1.6 %convert_reduce_fusion = f32[3200]{0:T(1024)S(1)} fusion(bf16[32,4,3200]{2,1,0:T(4,128)(2,1)} %get-tuple-element.8), kind=kLoop, calls=%fused_computation.4 | loop fusion | flops 816000 | bytes 832000 | tf_op jit(solution)/shard_map/reduce_sum | solution.py:242
  74.5 0.0 copy-start.2
  74.5 0.0 copy-start.3
  74.5 0.0 copy-start.4
  74.5 1.8 %multiply_reduce_fusion = f32[3200]{0:T(1024)S(1)} fusion(bf16[32,4,3200]{2,1,0:T(4,128)(2,1)} %get-tuple-element.8, f32[3200]{0:T(1024)S(1)} %broadcast_multiply_fusion), kind=kLoop, calls=%fused_computation.3 | loop fusion | flops 1635200 | bytes 844800 | tf_op jit(solution)/shard_map/reduce_sum | solution.py:244
  76.3 0.0 copy-done.1
  76.3 0.1 reshape.28
  76.5 0.0 copy-done
  76.5 0.0 copy-done.2
  76.5 0.0 copy-done.3
  76.5 0.0 copy-done.4
  76.5 1.4 %fusion = bf16[3200,128]{1,0:T(8,128)(2,1)} fusion(bf16[128,128]{1,0:T(8,128)(2,1)S(1)} %copy-done, bf16[3200,128]{1,0:T(8,128)(2,1)S(1)} %copy-done.2, f32[128,3200]{1,0:T(8,128)S(1)} %reshape.28, f32[128]{0:T(128)S(1)} %copy-done.3, f32[128]{0:T(128)S(1)} %copy-done.4, f32[3200]{0:T(1024)S(1)} %add_rsqrt_fusion, f32[3200]{0:T(1024)S(1)} %broadcast_multiply_fusion), kind=kOutput, calls=%fused_computation.1 | convolution fusion | flops 108134400 | bytes 3336192 | tf_op jit(solution)/shard_map/dot_general | solution.py:248
  (2 shorter events, 0.0 us)
Async XLA Ops:
  0.0 76.5 %copy-start = (bf16[128,128]{1,0:T(8,128)(2,1)S(1)}, bf16[128,128]{1,0:T(8,128)(2,1)}, u32[]{:S(2)}) copy-start(bf16[128,128]{1,0:T(8,128)(2,1)} %param.15) | copy-start | bytes 98308
  72.9 3.4 %copy-start.1 = (bf16[32,4,3200]{2,1,0:T(4,128)(2,1)S(1)}, bf16[32,4,3200]{2,1,0:T(4,128)(2,1)}, u32[]{:S(2)}) copy-start(bf16[32,4,3200]{2,1,0:T(4,128)(2,1)} %get-tuple-element.8) | copy-start | bytes 2457604
  74.5 2.0 %copy-start.2 = (bf16[3200,128]{1,0:T(8,128)(2,1)S(1)}, bf16[3200,128]{1,0:T(8,128)(2,1)}, u32[]{:S(2)}) copy-start(bf16[3200,128]{1,0:T(8,128)(2,1)} %get-tuple-element.7) | copy-start | bytes 2457604
  74.5 2.0 %copy-start.3 = (f32[128]{0:T(128)S(1)}, f32[128]{0:T(128)}, u32[]{:S(2)}) copy-start(f32[128]{0:T(128)} %param.14) | copy-start | bytes 1540
  74.5 2.0 %copy-start.4 = (f32[128]{0:T(128)S(1)}, f32[128]{0:T(128)}, u32[]{:S(2)}) copy-start(f32[128]{0:T(128)} %param.13) | copy-start | bytes 1540

commit v3 on v2

v3 whole, which is shorter than its diff:
```python
import functools

import jax
import jax.numpy as jnp
from jax import lax
from jax.experimental import pallas as pl
from jax.experimental.pallas import tpu as pltpu
from jax.sharding import PartitionSpec as P

MESH = pl.DeviceIdType.MESH
LANES = 128
PARTS = 2


def shifted(vregs, start):
    at, by = divmod(start, LANES)
    if by == 0:
        return vregs[at]
    return pltpu.roll(vregs[at], LANES - by, 1)


def body(n_ri, n_rj, rows, cols, parts, own, pair, gain, bias, w_in, w_gate, gate_ref, out_ref,
         flat_s, ab_s, x_s, recv_s, g_s, b_s, o_s, t_s,
         send1, recv1, send2, recv2, loc):
    n = n_ri * n_rj
    spots = rows * cols
    side = n_ri // 2
    team = n // 2
    depth = side * rows
    wide_part = team * own
    hidden = parts * wide_part
    halves = cols // rows
    ri, rj = lax.axis_index("ri"), lax.axis_index("rj")
    me = ri * n_rj + rj
    seat = lax.rem(ri, side) * n_rj + rj
    base = (ri // side) * side

    def other(d):
        return lax.rem(me + d, n)

    barrier = pltpu.get_barrier_semaphore()

    def greet(d, _):
        to = other(d)
        pl.semaphore_signal(
            barrier, inc=1, device_id=(to // n_rj, lax.rem(to, n_rj)), device_id_type=MESH
        )
        return _

    lax.fori_loop(1, n, greet, 0)

    wt = w_in[...].T
    step = spots // 5

    def project(i, _):
        at = pl.multiple_of(i * step, LANES)
        x = pair[pl.ds(at, step), :].astype(jnp.float32)
        mean = jnp.mean(x, axis=-1, keepdims=True)
        centered = x - mean
        var = jnp.mean(centered * centered, axis=-1, keepdims=True)
        flat = (centered * lax.rsqrt(var + 1e-05) * gain[...] + bias[...]).astype(jnp.bfloat16)
        flat_s[pl.ds(at, step), :] = flat
        proj = lax.dot_general(
            wt, flat, (((1,), (1,)), ((), ())), preferred_element_type=jnp.float32
        )
        ab_s[0, :, pl.ds(at, step)] = (
            jax.nn.sigmoid(proj[hidden : 2 * hidden]) * proj[:hidden]
        )
        ab_s[1, :, pl.ds(at, step)] = (
            jax.nn.sigmoid(proj[3 * hidden :]) * proj[2 * hidden : 3 * hidden]
        )
        return _

    lax.fori_loop(0, 5, project, 0)

    each = 8 // own

    def copy_in(t, d, src):
        return pltpu.make_async_remote_copy(
            src_ref=x_s.at[t, d], dst_ref=recv_s.at[t, src], send_sem=send1.at[t, d],
            recv_sem=recv1.at[t, src], device_id=(base + d // n_rj, lax.rem(d, n_rj)),
            device_id_type=MESH,
        )

    def copy_back(t, d, src):
        return pltpu.make_async_remote_copy(
            src_ref=t_s.at[t, d], dst_ref=out_ref.at[t, src], send_sem=send2.at[t, d],
            recv_sem=recv2.at[t, src], device_id=(d // n_rj, lax.rem(d, n_rj)),
            device_id_type=MESH,
        )

    for t in range(parts):
        def split(p, _):
            at = pl.multiple_of(t * wide_part + p * 8, 8)
            a8, b8 = ab_s[0, pl.ds(at, 8), :], ab_s[1, pl.ds(at, 8), :]
            for e in range(each):
                pick = slice(e * own, (e + 1) * own)
                x_s[t, p * each + e] = jnp.concatenate([a8[pick], b8[pick]], axis=0).astype(
                    jnp.bfloat16
                )
            return _

        lax.fori_loop(0, wide_part // 8, split, 0)
        if t == 0:
            pl.semaphore_wait(barrier, n - 1)

        def send(d, _):
            copy_in(t, lax.rem(seat + d, team), seat).start()
            return _

        lax.fori_loop(1, team, send, 0)

    def gates(i, _):
        at = pl.multiple_of(i * step, LANES)
        gate_ref[pl.ds(at, step), :] = jax.nn.sigmoid(
            jnp.dot(flat_s[pl.ds(at, step), :], w_gate[...], preferred_element_type=jnp.float32)
        ).astype(jnp.bfloat16)
        return _

    lax.fori_loop(0, 5, gates, 0)

    lane = lax.broadcasted_iota(jnp.int32, (2 * own, LANES), 1)

    def unpack(block, src):
        i0 = (src // n_rj) * rows
        j = lax.rem(src, n_rj)
        wide = block.astype(jnp.float32)
        vregs = [wide[:, v * LANES : (v + 1) * LANES] for v in range(spots // LANES)]
        for k in range(rows):
            start = k * cols
            val = shifted(vregs, start)
            have = LANES - start % LANES
            if have < cols:
                val = jnp.where(
                    lane < have, val, pltpu.roll(vregs[start // LANES + 1], have, 1)
                )
            g_s[j, pl.ds(i0 + k, 2 * own, stride=depth), :] = val

    lane_o = lax.broadcasted_iota(jnp.int32, (own, LANES), 1)

    for t in range(parts):
        unpack(x_s[t, seat], seat)

        def take(d, _):
            src = lax.rem(seat + team - d, team)
            copy_in(t, src, src).wait_recv()
            unpack(recv_s[t, src], src)
            return _

        lax.fori_loop(1, team, take, 0)

        for c in range(own):
            for q in range(n_rj):
                b_s[c, :, q * LANES : (q + 1) * LANES] = g_s[
                    q, (own + c) * depth : (own + c + 1) * depth, :
                ].astype(jnp.bfloat16)

        def emit(pp, _):
            p = lax.rem(pp + n_rj // 2 + ri // halves, n_rj)
            for c in range(own):
                lhs = g_s[p, c * depth : (c + 1) * depth, :].astype(jnp.bfloat16)
                product = lax.dot_general(
                    lhs, b_s[c], (((0,), (0,)), ((), ())), preferred_element_type=jnp.float32
                )
                for q in range(n_rj):
                    o_s[q, c * LANES : (c + 1) * LANES, :] = product[:, q * LANES : (q + 1) * LANES]

            def deliver(s, _):
                h, q = s // n_rj, lax.rem(s + rj, n_rj)
                d = (p * halves + h) * n_rj + q
                got = [
                    o_s[q, pl.ds(h * rows + r, own, stride=LANES), :] for r in range(rows)
                ]
                pieces = []
                for v in range(spots // LANES):
                    piece = None
                    for r in range((v * LANES) // cols, min(rows, ((v + 1) * LANES - 1) // cols + 1)):
                        at = r * cols - v * LANES
                        val = pltpu.roll(got[r], at % LANES, 1) if at % LANES else got[r]
                        piece = val if piece is None else jnp.where(lane_o >= at, val, piece)
                    pieces.append(piece)
                t_s[t, d] = jnp.concatenate(pieces, axis=1).astype(jnp.bfloat16)

                @pl.when(d != me)
                def start():
                    copy_back(t, d, me).start()

                return _

            lax.fori_loop(0, halves * n_rj, deliver, 0)
            return _

        lax.fori_loop(0, n_rj, emit, 0)
        pltpu.make_async_copy(t_s.at[t, me], out_ref.at[t, me], loc.at[t]).start()

    for t in range(parts):
        def sent(d, _):
            copy_in(t, lax.rem(seat + d, team), seat).wait_send()
            return _

        def finish(d, _):
            src = lax.rem(me + n - d, n)
            copy_back(t, other(d), me).wait_send()
            copy_back(t, src, src).wait_recv()
            return _

        lax.fori_loop(1, team, sent, 0)
        lax.fori_loop(1, n, finish, 0)
        pltpu.make_async_copy(t_s.at[t, me], out_ref.at[t, me], loc.at[t]).wait()


def exchange(n_ri, n_rj, rows, cols, parts, own, pair, gain, bias, w_in, w_gate):
    n = n_ri * n_rj
    spots, chans = pair.shape
    team = n // 2
    depth = (n_ri // 2) * rows
    hidden = parts * team * own
    vmem = pl.BlockSpec(memory_space=pltpu.VMEM)
    return pl.pallas_call(
        functools.partial(body, n_ri, n_rj, rows, cols, parts, own),
        out_shape=(
            jax.ShapeDtypeStruct((spots, chans), jnp.bfloat16),
            jax.ShapeDtypeStruct((parts, n, own, spots), jnp.bfloat16),
        ),
        in_specs=[vmem] * 5,
        out_specs=(vmem, vmem),
        scratch_shapes=[
            pltpu.VMEM((spots, chans), jnp.bfloat16),
            pltpu.VMEM((2, hidden, spots), jnp.float32),
            pltpu.VMEM((parts, team, 2 * own, spots), jnp.bfloat16),
            pltpu.VMEM((parts, team, 2 * own, spots), jnp.bfloat16),
            pltpu.VMEM((n_rj, 2 * own * depth, LANES), jnp.float32),
            pltpu.VMEM((own, depth, n_rj * LANES), jnp.bfloat16),
            pltpu.VMEM((n_rj, own * LANES, LANES), jnp.float32),
            pltpu.VMEM((parts, n, own, spots), jnp.bfloat16),
            pltpu.SemaphoreType.DMA((parts, team)),
            pltpu.SemaphoreType.DMA((parts, team)),
            pltpu.SemaphoreType.DMA((parts, n)),
            pltpu.SemaphoreType.DMA((parts, n)),
            pltpu.SemaphoreType.DMA((parts,)),
        ],
        compiler_params=pltpu.CompilerParams(
            collective_id=0, has_side_effects=True, vmem_limit_bytes=56 << 20
        ),
    )(pair, gain, bias, w_in, w_gate)


def local(n_ri, n_rj, pair, in_gain, in_bias, w_in, w_gate, out_gain, out_bias, w_out):
    rows, cols, chans = pair.shape
    hidden = w_out.shape[0]
    n = n_ri * n_rj
    team = n // 2
    parts = min(PARTS, hidden // team)
    own = hidden // (team * parts)
    spots = rows * cols
    gate, tri = exchange(
        n_ri, n_rj, rows, cols, parts, own, pair.reshape(spots, chans),
        in_gain[None], in_bias[None], w_in, w_gate,
    )
    tri = tri.reshape(parts, 2, team * own, spots).astype(jnp.float32)
    tri = (tri[:, 0] + tri[:, 1]).reshape(hidden, spots)
    mean = jnp.mean(tri, axis=0, keepdims=True)
    centered = tri - mean
    var = jnp.mean(centered * centered, axis=0, keepdims=True)
    tri_normed = (
        centered * lax.rsqrt(var + 1e-05) * out_gain[:, None] + out_bias[:, None]
    ).astype(jnp.bfloat16)
    mixed = lax.dot_general(
        tri_normed, w_out, (((0,), (0,)), ((), ())), preferred_element_type=jnp.float32
    )
    update = gate.astype(jnp.float32) * mixed
    return update.reshape(rows, cols, chans).astype(jnp.bfloat16)


def solution(mesh):
    n_ri, n_rj = mesh.shape["ri"], mesh.shape["rj"]
    return jax.shard_map(
        lambda *args: local(n_ri, n_rj, *args),
        mesh=mesh,
        in_specs=(P("ri", "rj", None), P(), P(), P(), P(), P(), P(), P()),
        out_specs=P("ri", "rj", None),
        check_vma=False,
    )
```

time: 78.1 us -> 65.7 us (0.84)
  the two profiles are of different devices: /device:TPU:1 before, /device:TPU:17 now
where the time goes in v3:
time: 65.7 us; the launch traced here: 65.5 us
  Pallas kernels  59.9 us (91%)
  local copies, waits for them, and re-layouts  3.46 us (5%)
  matrix products  1.31 us (2%)
  other arithmetic  0.71 us (1%)
    pallas_call x1, Pallas kernels, exchange(): pl.pallas_call(functools.partial(body, n_ri, n_rj, rows, cols, parts, own...  59.9 us
    convert_element_type x1, local copies, waits for them, and re-layouts, local(): tri = tri.reshape(parts, 2, team * own, spots).astype(jnp.float32)  2.66 us

profile of v3, /device:TPU:17, one launch (start us, length us, event | category | flops | bytes accessed | tf_op | source)
XLA Modules:
  0.0 65.5 jit_solution(10946689527714385446)
XLA Ops:
  0.0 0.0 copy-start
  0.0 59.9 %shard_map.82 = (bf16[3200,128]{1,0:T(8,128)(2,1)}, bf16[2,32,4,3200]{3,2,1,0:T(4,128)(2,1)}) custom-call(bf16[3200,128]{1,0:T(8,128)(2,1)} %bitcast.16, f32[1,128]{1,0:T(1,128)} %bitcast.17, f32[1,128]{1,0:T(1,128)} %bitcast.18, bf16[128,512]{1,0:T(8,128)(2,1)} %w_in.1, bf16[128,128]{1,0:T(8,128)(2,1)} %w_gate.1), custom_call_target="tpu_custom_call" | custom-call | tf_op jit(solution)/shard_map/pallas_call | solution.py:219
  59.9 2.7 %reshape.32 = f32[2,2,64,3200]{3,2,1,0:T(8,128)S(1)} reshape(bf16[2,32,4,3200]{3,2,1,0:T(4,128)(2,1)} %get-tuple-element.8) | data formatting | bytes 4915200 | tf_op jit(solution)/shard_map/convert_element_type | solution.py:260
  62.6 0.2 fusion.5
  62.8 0.0 copy-start.2
  62.8 0.0 copy-start.3
  62.8 0.2 multiply_reduce_fusion
  63.0 0.0 copy-start.1
  63.1 0.4 copy-done.2
  63.5 0.0 copy-done.3
  63.5 0.3 fusion.4
  63.8 0.0 copy-done
  63.8 0.4 copy-done.1
  64.2 1.3 %fusion = bf16[3200,128]{1,0:T(8,128)(2,1)} fusion(bf16[128,3200]{1,0:T(8,128)(2,1)S(1)} %fusion.4, bf16[128,128]{1,0:T(8,128)(2,1)S(1)} %copy-done, bf16[3200,128]{1,0:T(8,128)(2,1)S(1)} %copy-done.1), kind=kOutput, calls=%fused_computation.1 | convolution fusion | flops 106086400 | bytes 2490368 | tf_op jit(solution)/shard_map/dot_general | solution.py:268
  (2 shorter events, 0.0 us)
Async XLA Ops:
  0.0 63.8 %copy-start = (bf16[128,128]{1,0:T(8,128)(2,1)S(1)}, bf16[128,128]{1,0:T(8,128)(2,1)}, u32[]{:S(2)}) copy-start(bf16[128,128]{1,0:T(8,128)(2,1)} %param.15) | copy-start | bytes 98308
  62.8 0.7 %copy-start.2 = (f32[128]{0:T(128)S(1)}, f32[128]{0:T(128)}, u32[]{:S(2)}) copy-start(f32[128]{0:T(128)} %param.14) | copy-start | bytes 1540
  62.8 0.7 %copy-start.3 = (f32[128]{0:T(128)S(1)}, f32[128]{0:T(128)}, u32[]{:S(2)}) copy-start(f32[128]{0:T(128)} %param.13) | copy-start | bytes 1540
  63.0 1.1 %copy-start.1 = (bf16[3200,128]{1,0:T(8,128)(2,1)S(1)}, bf16[3200,128]{1,0:T(8,128)(2,1)}, u32[]{:S(2)}) copy-start(bf16[3200,128]{1,0:T(8,128)(2,1)} %get-tuple-element.7) | copy-start | bytes 2457604

commit v4 on v3

--- a/solution.py
+++ b/solution.py
@@ -19,8 +19,8 @@
     return pltpu.roll(vregs[at], LANES - by, 1)
 
 
-def body(n_ri, n_rj, rows, cols, parts, own, pair, gain, bias, w_in, w_gate, gate_ref, out_ref,
-         flat_s, ab_s, x_s, recv_s, g_s, b_s, o_s, t_s,
+def body(n_ri, n_rj, rows, cols, parts, own, pair, gain, bias, w_in, w_gate, gate_ref, tri_ref,
+         out_ref, flat_s, ab_s, x_s, recv_s, g_s, b_s, o_s, t_s,
          send1, recv1, send2, recv2, loc):
     n = n_ri * n_rj
     spots = rows * cols
@@ -204,9 +204,20 @@
             copy_back(t, src, src).wait_recv()
             return _
 
+        def merge(p, _):
+            at = pl.multiple_of(t * wide_part + p * 8, 8)
+            sums = [
+                out_ref[t, p * each + e].astype(jnp.float32)
+                + out_ref[t, team + p * each + e].astype(jnp.float32)
+                for e in range(each)
+            ]
+            tri_ref[pl.ds(at, 8), :] = jnp.concatenate(sums, axis=0)
+            return _
+
         lax.fori_loop(1, team, sent, 0)
         lax.fori_loop(1, n, finish, 0)
         pltpu.make_async_copy(t_s.at[t, me], out_ref.at[t, me], loc.at[t]).wait()
+        lax.fori_loop(0, wide_part // 8, merge, 0)
 
 
 def exchange(n_ri, n_rj, rows, cols, parts, own, pair, gain, bias, w_in, w_gate):
@@ -220,11 +231,12 @@
         functools.partial(body, n_ri, n_rj, rows, cols, parts, own),
         out_shape=(
             jax.ShapeDtypeStruct((spots, chans), jnp.bfloat16),
-            jax.ShapeDtypeStruct((parts, n, own, spots), jnp.bfloat16),
+            jax.ShapeDtypeStruct((hidden, spots), jnp.float32),
         ),
         in_specs=[vmem] * 5,
         out_specs=(vmem, vmem),
         scratch_shapes=[
+            pltpu.VMEM((parts, n, own, spots), jnp.bfloat16),
             pltpu.VMEM((spots, chans), jnp.bfloat16),
             pltpu.VMEM((2, hidden, spots), jnp.float32),
             pltpu.VMEM((parts, team, 2 * own, spots), jnp.bfloat16),
@@ -257,8 +269,6 @@
         n_ri, n_rj, rows, cols, parts, own, pair.reshape(spots, chans),
         in_gain[None], in_bias[None], w_in, w_gate,
     )
-    tri = tri.reshape(parts, 2, team * own, spots).astype(jnp.float32)
-    tri = (tri[:, 0] + tri[:, 1]).reshape(hidden, spots)
     mean = jnp.mean(tri, axis=0, keepdims=True)
     centered = tri - mean
     var = jnp.mean(centered * centered, axis=0, keepdims=True)

time: 65.7 us -> 63.8 us (0.971)
  the two profiles are of different devices: /device:TPU:17 before, /device:TPU:1 now
where the time goes in v4:
time: 63.8 us; the launch traced here: 62.6 us
  Pallas kernels  59 us (92%)
  other arithmetic  1.87 us (3%)
  matrix products  1.44 us (2%)
    pallas_call x1, Pallas kernels, exchange(): pl.pallas_call(functools.partial(body, n_ri, n_rj, rows, cols, parts, own...  59 us
    reduce_sum x1, other arithmetic, local(): mean = jnp.mean(tri, axis=0, keepdims=True)  1.67 us
    dot_general x1, matrix products, local(): lax.dot_general(tri_normed, w_out, (((0,), (0,)), ((), ())), preferred_el...  1.44 us

profile of v4, /device:TPU:1, one launch (start us, length us, event | category | flops | bytes accessed | tf_op | source)
XLA Modules:
  0.0 62.6 jit_solution(3510992495286299436)
XLA Ops:
  0.0 0.0 copy-start
  0.0 59.0 %shard_map.82 = (bf16[3200,128]{1,0:T(8,128)(2,1)}, f32[128,3200]{1,0:T(8,128)}) custom-call(bf16[3200,128]{1,0:T(8,128)(2,1)} %bitcast.5, f32[1,128]{1,0:T(1,128)} %bitcast.6, f32[1,128]{1,0:T(1,128)} %bitcast.7, bf16[128,512]{1,0:T(8,128)(2,1)} %w_in.1, bf16[128,128]{1,0:T(8,128)(2,1)} %w_gate.1), custom_call_target="tpu_custom_call" | custom-call | tf_op jit(solution)/shard_map/pallas_call | solution.py:230
  59.0 0.0 copy-start.1
  59.0 0.0 copy-start.2
  59.0 0.0 copy-start.3
  59.0 0.0 copy-start.4
  59.0 1.7 %reduce_sum.18 = f32[3200]{0:T(1024)S(1)} reduce(f32[128,3200]{1,0:T(8,128)} %get-tuple-element.8, f32[]{:T(128)} %constant.2.clone.1), dimensions={0}, to_apply=%region_0.0 | reduce | flops 406400 | bytes 1651204 | tf_op jit(solution)/shard_map/reduce_sum | solution.py:272
  60.7 0.2 copy-done.1
  60.9 0.2 multiply_reduce_fusion
  61.1 0.0 copy-done
  61.1 0.0 copy-done.2
  61.1 0.0 copy-done.3
  61.1 0.0 copy-done.4
  61.1 1.4 %fusion = bf16[3200,128]{1,0:T(8,128)(2,1)} fusion(bf16[128,128]{1,0:T(8,128)(2,1)S(1)} %copy-done, bf16[3200,128]{1,0:T(8,128)(2,1)S(1)} %copy-done.2, f32[128,3200]{1,0:T(8,128)S(1)} %copy-done.1, f32[128]{0:T(128)S(1)} %copy-done.3, f32[128]{0:T(128)S(1)} %copy-done.4, f32[3200]{0:T(1024)S(1)} %add_rsqrt_fusion, f32[3200]{0:T(1024)S(1)} %broadcast_multiply_fusion), kind=kOutput, calls=%fused_computation.1 | convolution fusion | flops 108134400 | bytes 3336192 | tf_op jit(solution)/shard_map/dot_general | solution.py:278
  (2 shorter events, 0.0 us)
Async XLA Ops:
  0.0 61.1 %copy-start = (bf16[128,128]{1,0:T(8,128)(2,1)S(1)}, bf16[128,128]{1,0:T(8,128)(2,1)}, u32[]{:S(2)}) copy-start(bf16[128,128]{1,0:T(8,128)(2,1)} %param.15) | copy-start | bytes 98308
  59.0 1.9 %copy-start.1 = (f32[128,3200]{1,0:T(8,128)S(1)}, f32[128,3200]{1,0:T(8,128)}, u32[]{:S(2)}) copy-start(f32[128,3200]{1,0:T(8,128)} %get-tuple-element.8) | copy-start | bytes 4915204
  59.0 2.1 %copy-start.2 = (bf16[3200,128]{1,0:T(8,128)(2,1)S(1)}, bf16[3200,128]{1,0:T(8,128)(2,1)}, u32[]{:S(2)}) copy-start(bf16[3200,128]{1,0:T(8,128)(2,1)} %get-tuple-element.7) | copy-start | bytes 2457604
  59.0 2.1 %copy-start.3 = (f32[128]{0:T(128)S(1)}, f32[128]{0:T(128)}, u32[]{:S(2)}) copy-start(f32[128]{0:T(128)} %param.14) | copy-start | bytes 1540
  59.0 2.1 %copy-start.4 = (f32[128]{0:T(128)S(1)}, f32[128]{0:T(128)}, u32[]{:S(2)}) copy-start(f32[128]{0:T(128)} %param.13) | copy-start | bytes 1540

commit v5 on v4

--- a/solution.py
+++ b/solution.py
@@ -218,6 +218,17 @@
         lax.fori_loop(1, n, finish, 0)
         pltpu.make_async_copy(t_s.at[t, me], out_ref.at[t, me], loc.at[t]).wait()
         lax.fori_loop(0, wide_part // 8, merge, 0)
+
+    def normalize(i, _):
+        at = pl.multiple_of(i * step, LANES)
+        x = tri_ref[:, pl.ds(at, step)]
+        mean = jnp.mean(x, axis=0, keepdims=True)
+        centered = x - mean
+        var = jnp.mean(centered * centered, axis=0, keepdims=True)
+        tri_ref[:, pl.ds(at, step)] = centered * lax.rsqrt(var + 1e-05)
+        return _
+
+    lax.fori_loop(0, 5, normalize, 0)
 
 
 def exchange(n_ri, n_rj, rows, cols, parts, own, pair, gain, bias, w_in, w_gate):
@@ -269,12 +280,7 @@
         n_ri, n_rj, rows, cols, parts, own, pair.reshape(spots, chans),
         in_gain[None], in_bias[None], w_in, w_gate,
     )
-    mean = jnp.mean(tri, axis=0, keepdims=True)
-    centered = tri - mean
-    var = jnp.mean(centered * centered, axis=0, keepdims=True)
-    tri_normed = (
-        centered * lax.rsqrt(var + 1e-05) * out_gain[:, None] + out_bias[:, None]
-    ).astype(jnp.bfloat16)
+    tri_normed = (tri * out_gain[:, None] + out_bias[:, None]).astype(jnp.bfloat16)
     mixed = lax.dot_general(
         tri_normed, w_out, (((0,), (0,)), ((), ())), preferred_element_type=jnp.float32
     )

time: 63.8 us -> 63.7 us (level)
  the two profiles are of different devices: /device:TPU:1 before, /device:TPU:17 now
where the time goes in v5:
time: 63.7 us; the launch traced here: 63.6 us
  Pallas kernels  60.5 us (95%)
  matrix products  3.07 us (5%)
    pallas_call x1, Pallas kernels, exchange(): pl.pallas_call(functools.partial(body, n_ri, n_rj, rows, cols, parts, own...  60.5 us
    dot_general x1, matrix products, local(): lax.dot_general(tri_normed, w_out, (((0,), (0,)), ((), ())), preferred_el...  3.07 us

profile of v5, /device:TPU:17, one launch (start us, length us, event | category | flops | bytes accessed | tf_op | source)
XLA Modules:
  0.0 63.6 jit_solution(2693583903835240220)
XLA Ops:
  0.0 0.0 copy-start
  0.0 60.5 %shard_map.82 = (bf16[3200,128]{1,0:T(8,128)(2,1)}, f32[128,3200]{1,0:T(8,128)}) custom-call(bf16[3200,128]{1,0:T(8,128)(2,1)} %bitcast.5, f32[1,128]{1,0:T(1,128)} %bitcast.6, f32[1,128]{1,0:T(1,128)} %bitcast.7, bf16[128,512]{1,0:T(8,128)(2,1)} %w_in.1, bf16[128,128]{1,0:T(8,128)(2,1)} %w_gate.1), custom_call_target="tpu_custom_call" | custom-call | tf_op jit(solution)/shard_map/pallas_call | solution.py:241
  60.5 0.0 copy-done
  60.5 3.1 %fusion = bf16[3200,128]{1,0:T(8,128)(2,1)} fusion(bf16[128,128]{1,0:T(8,128)(2,1)S(1)} %copy-done, bf16[3200,128]{1,0:T(8,128)(2,1)} %get-tuple-element.7, f32[128,3200]{1,0:T(8,128)} %get-tuple-element.8, f32[128]{0:T(128)} %param.14, f32[128]{0:T(128)} %param.13), kind=kOutput, calls=%fused_computation.1 | convolution fusion | flops 107315200 | bytes 3310592 | tf_op jit(solution)/shard_map/dot_general | solution.py:284
Async XLA Ops:
  0.0 60.5 %copy-start = (bf16[128,128]{1,0:T(8,128)(2,1)S(1)}, bf16[128,128]{1,0:T(8,128)(2,1)}, u32[]{:S(2)}) copy-start(bf16[128,128]{1,0:T(8,128)(2,1)} %param.15) | copy-start | bytes 98308
